TPU v7x, 32 devices: a whole 2x2x4 slice. The times are simulated.
32 devices in a mesh: region: 4 (over z), tracer: 2 (over x), sect: 4 (over y, core).
Axes of the slice: x: 2, y: 2, z: 4, core: 2. Of those that a mesh axis runs over, the one named last changes fastest.
Arguments:
- solute_concentration: float32 [16, 96, 32, 128], P('tracer', 'region', 'sect'), may hold values from 0.5 to 2
- thermal_anomaly: float32 [96, 32, 128], P('region', 'sect'), may hold values from -6 to 6
- eastward_flow_speed: float32 [96, 32, 128], P('region', 'sect'), may hold values from -1 to 1
- northward_flow_speed: float32 [96, 32, 128], P('region', 'sect'), may hold values from -1 to 1
- submerged_layers: int32 [96, 32], P('region', 'sect'), may hold values from 0 to 128, as said below
- interaction_matrix: float32 [16, 16], replicated, may hold values from -1.5 to 1.5
- bloom_yields: float32 [16], replicated, may hold values from -8 to 8
Outputs:
- tracers_next: float32 [16, 96, 32, 128], P('tracer', 'region', 'sect')
- temperature_next: float32 [96, 32, 128], P('region', 'sect')
Inputs may be any that keep to these rules, and one draw needn't show every extreme that they name: `submerged_layers`: land (0) forms a few contiguous masses, with shallow shelves around them; columns far from land have all 128 levels.
All inputs are finite; a program needn't handle non-finite values.
Results may differ from a plain program's by a relative error of at most 0.0001.
Values sent between devices are 32-bit elements; how exact they have to be, the bound alone decides.
A program may use at most 64 MiB of HBM per device.

v0:
```python
import functools

import jax
import jax.numpy as jnp
from jax import lax
from jax.experimental import pallas as pl
from jax.experimental.pallas import tpu as pltpu
from jax.sharding import PartitionSpec as P

STEPS = 3
SUB = 4

TIME_STEP = 0.2
REACT_STEP = 0.1
GROWTH_MAX = 1.0
HALF_SAT = 0.5
WATER_ATT = 3.0
CHL_ATT = 2.0
HEAT_GAIN = 0.5

MESH = pl.DeviceIdType.MESH
HIGHEST = lax.Precision.HIGHEST
EAST, WEST, NORTH, SOUTH = range(4)


def iota(shape, dim):
    return lax.broadcasted_iota(jnp.int32, shape, dim)


def exact_dot(a, b, dims=((1,), (0,))):
    return lax.dot_general(
        a, b, (dims, ((), ())), precision=HIGHEST, preferred_element_type=jnp.float32
    )


def halves(x):
    high = x.astype(jnp.bfloat16)
    return high, (x - high.astype(jnp.float32)).astype(jnp.bfloat16)


def half_dot(a, b):
    return jnp.dot(a, b, preferred_element_type=jnp.float32)


def dot3(a, b):
    return half_dot(a[0], b[0]) + half_dot(a[1], b[0]) + half_dot(a[0], b[1])


def tables(rates_ref, yields_ref, tracers, wide, Y):
    rows = tracers * Y
    spread = (iota((rows, tracers), 0) // Y == iota((rows, tracers), 1)).astype(jnp.float32)
    same = iota((rows, rows), 0) % Y == iota((rows, rows), 1) % Y
    full = exact_dot(exact_dot(spread, rates_ref[...]), spread, ((1,), (1,)))
    full = jnp.where(same, full, 0.0) * REACT_STEP
    diagonal = (iota((rows, rows), 0) == iota((rows, rows), 1)).astype(jnp.float32)
    one = diagonal + full
    two = exact_dot(one, one)
    three = exact_dot(two, one)
    four = exact_dot(two, two)
    source = [
        exact_dot(spread * yields_ref[...], jnp.ones((tracers, wide), jnp.float32)) * REACT_STEP
    ]
    for power in (one, two, three):
        source.append(exact_dot(power, source[0]))
    head = jnp.concatenate([power[: 3 * Y] for power in (one, two, three)], axis=0)
    shape = (rows, wide)
    lane = iota(shape, 1)
    inject = jnp.zeros(shape, jnp.float32)
    for sub in range(SUB):
        hit = jnp.logical_and(lane // Y == sub, lane % Y == iota(shape, 0) % Y)
        inject = inject + jnp.where(hit, source[SUB - 1 - sub], 0.0)
    return head, four, inject[:, : SUB * Y], [v[: 3 * Y] for v in source[: SUB - 1]]


def stack(flat, wide):
    return jnp.concatenate(
        [flat[:, i * wide : (i + 1) * wide] for i in range(flat.shape[1] // wide)], axis=0
    )


def unstack(tall, Y):
    return jnp.concatenate(
        [tall[i * Y : (i + 1) * Y] for i in range(tall.shape[0] // Y)], axis=1
    )


def plan(span):
    return (3, (0, 2, 1)) if span % 3 == 0 else (1, (0,))


def kernel(
    regions, groups, sects,
    solute, heat_hbm, east_hbm, north_hbm, layers_hbm, rates_hbm, yields_hbm,
    tracers_out, heat_out,
    layers_in, rates_ref, yields_ref,
    state, ysend, yrecv, coef, final,
    in_send, in_recv, halo_send, halo_recv, out_send, out_recv, local_sem, load_sem,
):
    region, group, sect = (lax.axis_index(a) for a in ("region", "tracer", "sect"))
    own, wide, Y = solute.shape[0], solute.shape[2], layers_in.shape[0]
    tracers = own * groups
    block = heat_hbm.shape[0] // groups
    span = block // Y
    fields = tracers + 1
    every = fields + 3

    def place(reg, t):
        return t + (reg % 2) * (groups - 1 - 2 * t)

    part = place(region, group)
    last = groups - 1
    next_region = lax.rem(region + 1, regions)
    past_region = lax.rem(region + regions - 1, regions)
    east_region = jnp.where(part == last, next_region, region)
    west_region = jnp.where(part == 0, past_region, region)
    east_part = jnp.where(part == last, 0, part + 1)
    west_part = jnp.where(part == 0, last, part - 1)
    beside = {
        EAST: {"region": east_region, "tracer": place(east_region, east_part)},
        WEST: {"region": west_region, "tracer": place(west_region, west_part)},
        NORTH: {"sect": lax.rem(sect + 1, sects)},
        SOUTH: {"sect": lax.rem(sect + sects - 1, sects)},
    }
    peers = [lax.rem(group + d, groups) for d in range(1, groups)]

    def rows_of(t):
        return pl.ds(pl.multiple_of(place(region, t) * block, Y), block)

    mine = rows_of(group)
    slot = pl.ds(group * own, own)
    inner = pl.ds(Y, block)

    barrier = pltpu.get_barrier_semaphore()
    for peer in peers:
        pl.semaphore_signal(barrier, inc=1, device_id={"tracer": peer}, device_id_type=MESH)
    for side in range(4):
        pl.semaphore_signal(barrier, inc=1, device_id=beside[side], device_id_type=MESH)
    keep = pltpu.make_async_copy(
        solute.at[:, mine, :], state.at[0, slot, inner, :], local_sem.at[0, 0]
    )
    keep.start()
    loads = []
    for i, (source_ref, target_ref) in enumerate(
        (
            (layers_hbm, layers_in),
            (rates_hbm, rates_ref),
            (yields_hbm, yields_ref),
            (heat_hbm.at[mine, :], state.at[0, tracers, inner, :]),
            (east_hbm.at[mine, :], state.at[0, fields, inner, :]),
            (north_hbm.at[mine, :], state.at[0, fields + 1, inner, :]),
        )
    ):
        copy = pltpu.make_async_copy(source_ref, target_ref, load_sem.at[i])
        copy.start()
        loads.append(copy)
    pl.semaphore_wait(barrier, groups - 1 + 4)

    chunks, order = plan(span)
    deep = span // chunks
    piece = deep * Y

    def part_of(t, c):
        return pl.ds(pl.multiple_of(place(region, t) * block + c * piece, Y), piece)

    arriving = {}
    for i, c in enumerate(order):
        for d, peer in enumerate(peers):
            copy = pltpu.make_async_remote_copy(
                src_ref=solute.at[:, part_of(peer, c), :],
                dst_ref=state.at[0, slot, pl.ds(Y + c * piece, piece), :],
                send_sem=in_send.at[d, c],
                recv_sem=in_recv.at[d, c],
                device_id={"tracer": peer},
                device_id_type=MESH,
            )
            copy.start()
            arriving[c, d] = copy

    for copy in loads:
        copy.wait()
    total = layers_in.shape[1] * Y
    pick = (iota((total, layers_in.shape[1]), 0) // Y == iota((total, layers_in.shape[1]), 1))
    depth = lax.dot_general(
        pick.astype(jnp.bfloat16),
        layers_in[...].astype(jnp.float32).astype(jnp.bfloat16),
        (((1,), (1,)), ((), ())),
        preferred_element_type=jnp.float32,
    )
    depth = jnp.where(iota((total, Y), 0) % Y == iota((total, Y), 1), depth, 0.0)
    depth = half_dot(depth.astype(jnp.bfloat16), jnp.ones((Y, wide), jnp.bfloat16))
    coef[5] = (iota((total, wide), 1).astype(jnp.float32) < depth).astype(jnp.float32)
    state[0, fields + 2, inner, :] = coef[5, mine, :]

    head, four, inject, source = tables(rates_ref, yields_ref, tracers, wide, Y)
    head, four, inject = halves(head), halves(four), halves(inject)
    upper = (iota((wide, wide), 0) < iota((wide, wide), 1)).astype(jnp.bfloat16)
    level = iota((piece, wide), 1).astype(jnp.float32) + 0.5
    tile = (1, deep)
    source = [jnp.tile(v, tile) for v in source]

    def light(chl_abs):
        high, low = halves(chl_abs)
        above = half_dot(high, upper) + half_dot(low, upper)
        return jnp.exp(
            -(WATER_ATT / wide * level + CHL_ATT / wide * (above + 0.5 * chl_abs))
        )

    sent = []

    def exchange(step, c):
        count = every if step == 0 else fields
        some = pl.ds(0, count)
        moves = {}
        if c == chunks - 1:
            moves[EAST] = (
                state.at[step, some, pl.ds(block, Y), :],
                state.at[step, some, pl.ds(0, Y), :],
            )
        if c == 0:
            moves[WEST] = (
                state.at[step, some, pl.ds(Y, Y), :],
                state.at[step, some, pl.ds(block + Y, Y), :],
            )

        def send(moves):
            for side, (source_ref, target_ref) in moves.items():
                copy = pltpu.make_async_remote_copy(
                    src_ref=source_ref,
                    dst_ref=target_ref,
                    send_sem=halo_send.at[step, c, side],
                    recv_sem=halo_recv.at[step, c, side],
                    device_id=beside[side],
                    device_id_type=MESH,
                )
                copy.start()
                sent.append(copy)
                halos[step, c, side] = copy

        send(moves)
        for f in range(count):
            for side, y in ((0, 0), (1, Y - 1)):
                ysend[step, c, side, f] = state[
                    step, f, pl.ds(Y + c * piece + y, deep, stride=Y), :
                ]
        moves = {
            NORTH: (ysend.at[step, c, 1, some], yrecv.at[step, c, 1, some]),
            SOUTH: (ysend.at[step, c, 0, some], yrecv.at[step, c, 0, some]),
        }
        send(moves)

    halos = {}

    def beside_y(step, value, x, first, count):
        at = (count, Y, wide)
        row = iota(at, 1)
        some = pl.ds(first, count)
        above = jnp.broadcast_to(yrecv[step, x // deep, 0, some, pl.ds(x % deep, 1), :], at)
        below = jnp.broadcast_to(yrecv[step, x // deep, 1, some, pl.ds(x % deep, 1), :], at)
        up = jnp.where(row == Y - 1, above, pltpu.roll(value, Y - 1, 1))
        down = jnp.where(row == 0, below, pltpu.roll(value, 1, 1))
        return up, down

    keep.wait()
    for c in order:
        for d in range(len(peers)):
            arriving[c, d].wait_recv()
        exchange(0, c)

    leaving = []

    def leave(c):
        rows = pl.ds(c * piece, piece)
        out_rows = part_of(group, c)
        for d, peer in enumerate(peers):
            pairs = (
                (final.at[pl.ds(peer * own, own), rows, :], tracers_out.at[:, out_rows, :]),
                (final.at[tracers, rows, :], heat_out.at[out_rows, :]),
            )
            for i, (source_ref, target_ref) in enumerate(pairs):
                copy = pltpu.make_async_remote_copy(
                    src_ref=source_ref,
                    dst_ref=target_ref,
                    send_sem=out_send.at[d, c, i],
                    recv_sem=out_recv.at[d, c, i],
                    device_id={"tracer": peer},
                    device_id_type=MESH,
                )
                copy.start()
                leaving.append(copy)
        pairs = (
            (final.at[slot, rows, :], tracers_out.at[:, out_rows, :]),
            (final.at[tracers, rows, :], heat_out.at[out_rows, :]),
        )
        for i, (source_ref, target_ref) in enumerate(pairs):
            copy = pltpu.make_async_copy(source_ref, target_ref, local_sem.at[c, 1 + i])
            copy.start()
            leaving.append(copy)

    def advance(step, c):
        columns, heats, wets = [], [], []
        for x in range(c * deep, (c + 1) * deep):
            here = pl.ds((x + 1) * Y, Y)
            ahead = pl.ds((x + 2) * Y, Y)
            behind = pl.ds(x * Y, Y)
            cell = pl.ds(x * Y, Y)
            if step == 0:
                speed_wet = state[0, pl.ds(fields + 1, 2), here, :]
                up, down = beside_y(0, speed_wet, x, fields + 1, 2)
                wet = speed_wet[1]
                east = state[0, fields, here, :] * wet * state[0, fields + 2, ahead, :]
                west = state[0, fields, behind, :] * state[0, fields + 2, behind, :] * wet
                north = speed_wet[0] * wet * up[1]
                south = down[0] * down[1] * wet
                scaled = TIME_STEP * wet
                coef[0, cell, :] = wet - scaled * (
                    jnp.maximum(east, 0.0) - jnp.minimum(west, 0.0)
                    + jnp.maximum(north, 0.0) - jnp.minimum(south, 0.0)
                )
                coef[1, cell, :] = -scaled * jnp.minimum(east, 0.0)
                coef[2, cell, :] = scaled * jnp.maximum(west, 0.0)
                coef[3, cell, :] = -scaled * jnp.minimum(north, 0.0)
                coef[4, cell, :] = scaled * jnp.maximum(south, 0.0)
            value = state[step, pl.ds(0, fields), here, :]
            up, down = beside_y(step, value, x, 0, fields)
            moved = (
                coef[0, cell, :] * value
                + coef[1, cell, :] * state[step, pl.ds(0, fields), ahead, :]
                + coef[2, cell, :] * state[step, pl.ds(0, fields), behind, :]
                + coef[3, cell, :] * up
                + coef[4, cell, :] * down
            )
            columns.append(moved[:tracers].reshape(tracers * Y, wide))
            heats.append(moved[tracers])
            wets.append(state[0, fields + 2, here, :])
        mixed = jnp.concatenate(columns, axis=1)
        parts = halves(mixed)
        ahead_rows = dot3(head, parts)
        result = dot3(four, parts)
        rates = []
        for sub in range(SUB):
            if sub == 0:
                rows = mixed[: 3 * Y]
            else:
                rows = ahead_rows[(sub - 1) * 3 * Y : sub * 3 * Y]
                for i, rate in enumerate(rates):
                    rows = rows + source[sub - 1 - i] * jnp.concatenate([rate] * 3, axis=0)
            nutrient, chl, phyto = rows[:Y], rows[Y : 2 * Y], rows[2 * Y :]
            shade = unstack(light(jnp.abs(stack(chl, wide))), Y)
            rates.append(
                GROWTH_MAX * shade * nutrient / (jnp.abs(nutrient) + HALF_SAT) * phyto
            )
        result = result + dot3(inject, halves(jnp.concatenate(rates, axis=0)))
        chl_abs = jnp.abs(stack(result[Y : 2 * Y], wide))
        heating = HEAT_GAIN * chl_abs * light(chl_abs)
        heat = jnp.concatenate(heats, axis=0) + TIME_STEP * jnp.concatenate(wets, axis=0) * heating
        if step < STEPS - 1:
            target, base = state.at[step + 1], Y + c * piece
        else:
            target, base = final, c * piece
        for x in range(deep):
            target[pl.ds(0, tracers), pl.ds(base + x * Y, Y), :] = result[
                :, x * wide : (x + 1) * wide
            ].reshape(tracers, Y, wide)
        target[tracers, pl.ds(base, piece), :] = heat

    for step in range(STEPS):
        for c in order:
            for side in (NORTH, SOUTH):
                halos[step, c, side].wait_recv()
            if c == 0:
                halos[step, chunks - 1, EAST].wait_recv()
            if c == chunks - 1:
                halos[step, 0, WEST].wait_recv()
            advance(step, c)
            if step < STEPS - 1:
                exchange(step + 1, c)
            else:
                leave(c)
    for copy in leaving:
        copy.wait()
    for copy in sent + list(arriving.values()):
        copy.wait_send()

SHARE = 0
FIRST = 3


def wide_halves(x):
    high, low = halves(x)
    return jnp.concatenate([high, high, low], axis=1)


def tall_halves(x):
    high, low = halves(x)
    return jnp.concatenate([high, low, high], axis=0)


def pair_tables(rates_ref, yields_ref, tracers, wide, Y):
    rows = tracers * Y
    spread = (iota((rows, tracers), 0) // Y == iota((rows, tracers), 1)).astype(jnp.float32)
    same = iota((rows, rows), 0) % Y == iota((rows, rows), 1) % Y
    full = exact_dot(exact_dot(spread, rates_ref[...]), spread, ((1,), (1,)))
    full = jnp.where(same, full, 0.0) * REACT_STEP
    diagonal = (iota((rows, rows), 0) == iota((rows, rows), 1)).astype(jnp.float32)
    one = diagonal + full
    two = exact_dot(one, one)
    three = exact_dot(two, one)
    four = exact_dot(two, two)
    source = [
        exact_dot(spread * yields_ref[...], jnp.ones((tracers, wide), jnp.float32)) * REACT_STEP
    ]
    for power in (one, two, three):
        source.append(exact_dot(power, source[0]))
    powers = jnp.concatenate([power[: 3 * Y] for power in (one, two, three)] + [four], axis=0)
    shape = (rows, wide)
    lane = iota(shape, 1)
    inject = jnp.zeros(shape, jnp.float32)
    for sub in range(SUB):
        hit = jnp.logical_and(lane // Y == sub, lane % Y == iota(shape, 0) % Y)
        inject = inject + jnp.where(hit, source[SUB - 1 - sub], 0.0)
    return (
        wide_halves(powers),
        wide_halves(inject[:, : SUB * Y]),
        [v[: 3 * Y] for v in source],
    )


def pair_plan(half):
    low = -SHARE - STEPS
    ranges, at = [(half - STEPS, STEPS)], SHARE - STEPS
    while at < half - STEPS:
        size = min(STEPS, half - STEPS - at)
        ranges.append((at, size))
        at += size
    if SHARE:
        ranges.append((low, SHARE * 2))
    return low, ranges


def pair_kernel(
    regions, sects,
    solute, heat_hbm, east_hbm, north_hbm, layers_hbm, rates_hbm, yields_hbm,
    tracers_out, heat_out,
    layers_in, rates_ref, yields_ref, state, coef, wets, final,
    send_sem, recv_sem, local_sem,
):
    groups = 2
    region, group, sect = (lax.axis_index(a) for a in ("region", "tracer", "sect"))
    own, X, Y, wide = solute.shape
    half = X // groups
    tracers = own * groups
    fields = tracers + 1
    base = STEPS + 1
    low, ranges = pair_plan(half)
    reach = half - low
    odd = region % 2
    part = group + odd * (1 - 2 * group)
    peer = 1 - group

    def pick(flag, a, b):
        return a + flag * (b - a)

    def P(u, k, flag=part):
        return pick(flag, half + STEPS - u - k, u - low)

    def B(u, k, flag=part):
        return pick(flag, half - u - k, half + u)

    outer_region = lax.rem(region + pick(part, regions - 1, 1), regions)
    outer_part = 1 - part
    outer_odd = outer_region % 2
    beside = {"region": outer_region, "tracer": outer_part + outer_odd * (1 - 2 * outer_part)}
    north = {"sect": lax.rem(sect + 1, sects)}
    south = {"sect": lax.rem(sect + sects - 1, sects)}
    across = {"tracer": peer}
    mine, other = pl.ds(group * own, own), pl.ds(peer * own, own)

    barrier = pltpu.get_barrier_semaphore()
    for device in (across, beside, north, south):
        pl.semaphore_signal(barrier, inc=1, device_id=device, device_id_type=MESH)

    count = [0, 0]
    sent, leaving, arrivals = [], [], []

    def local(source_ref, target_ref):
        copy = pltpu.make_async_copy(source_ref, target_ref, local_sem.at[count[0]])
        count[0] += 1
        copy.start()
        return copy

    def remote(source_ref, target_ref, device):
        copy = pltpu.make_async_remote_copy(
            src_ref=source_ref,
            dst_ref=target_ref,
            send_sem=send_sem.at[count[1]],
            recv_sem=recv_sem.at[count[1]],
            device_id=device,
            device_id_type=MESH,
        )
        count[1] += 1
        copy.start()
        sent.append(copy)
        return copy

    raw = state.at[0]
    body = pl.ds(base, Y)
    tables_in = [
        local(layers_hbm, layers_in),
        local(rates_hbm, rates_ref),
        local(yields_hbm, yields_ref),
    ]
    p_all, b_all = P(low, reach), B(low, reach)
    in_block = pl.ds(b_all, reach)
    in_state = pl.ds(p_all, reach)
    extra = ((heat_hbm, tracers), (east_hbm, fields), (north_hbm, fields + 1))
    loads = [local(solute.at[:, in_block], raw.at[mine, in_state, body])]
    for ref, field in extra:
        loads.append(local(ref.at[in_block], raw.at[field, in_state, body]))

    with jax.named_scope('barrier'):
        pl.semaphore_wait(barrier, 4)

    def cross(u, k):
        return remote(
            solute.at[:, pl.ds(B(u, k, 1 - part), k)],
            raw.at[mine, pl.ds(P(u, k, 1 - part), k), body],
            across,
        )

    edge = half - STEPS
    edge_block = pl.ds(B(edge, STEPS), STEPS)
    edge_state = pl.ds(P(edge, STEPS), STEPS)
    past = pl.ds(pick(part, reach, 0), STEPS)
    crossing = [cross(*ranges[0])]
    outer = [remote(solute.at[:, edge_block], raw.at[mine, past, body], beside)]
    for ref, field in extra:
        outer.append(remote(ref.at[edge_block], raw.at[field, past, body], beside))
    crossing += [cross(*r) for r in ranges[1:]]
    sides = (
        (pl.ds(Y - STEPS, STEPS), pl.ds(base - STEPS, STEPS), north),
        (pl.ds(0, STEPS), pl.ds(base + Y, STEPS), south),
    )
    rows = []
    for block_rows, halo_rows, device in sides:
        rows.append(
            remote(
                solute.at[:, in_block, block_rows], raw.at[mine, in_state, halo_rows], device
            )
        )
        for ref, field in extra:
            rows.append(
                remote(ref.at[in_block, block_rows], raw.at[field, in_state, halo_rows], device)
            )

    def beside_rows(some, place):
        return [
            remote(
                raw.at[some, place, pl.ds(base + y, STEPS)],
                raw.at[some, place, halo_rows],
                device,
            )
            for y, (_, halo_rows, device) in zip((Y - STEPS, 0), sides)
        ]

    for copy in tables_in:
        copy.wait()
    total = X * Y
    pick_rows = iota((total, X), 0) // Y == iota((total, X), 1)
    depth = lax.dot_general(
        pick_rows.astype(jnp.bfloat16),
        layers_in[...].astype(jnp.float32).astype(jnp.bfloat16),
        (((1,), (1,)), ((), ())),
        preferred_element_type=jnp.float32,
    )
    depth = jnp.where(iota((total, Y), 0) % Y == iota((total, Y), 1), depth, 0.0)
    depth = half_dot(depth.astype(jnp.bfloat16), jnp.ones((Y, wide), jnp.bfloat16))
    wets[...] = (iota((total, wide), 1).astype(jnp.float32) < depth).astype(jnp.float32).reshape(
        X, Y, wide
    )
    wet_field = fields + 2
    raw[wet_field, in_state, body, :] = wets[in_block]
    outer.append(remote(raw.at[wet_field, edge_state, body], raw.at[wet_field, past, body], beside))
    rows += beside_rows(wet_field, in_state)

    with jax.named_scope('tables'):
        powers, inject, source = pair_tables(rates_ref, yields_ref, tracers, wide, Y)
    shape = (wide, wide)
    upper = (iota(shape, 0) < iota(shape, 1)).astype(jnp.float32)
    upper = upper + 0.5 * (iota(shape, 0) == iota(shape, 1)).astype(jnp.float32)
    upper = jnp.concatenate([upper.astype(jnp.bfloat16)] * 2, axis=0)
    level = (iota((Y, wide), 1).astype(jnp.float32) + 0.5) * (-WATER_ATT / wide)
    for copy in loads:
        copy.wait()

    def light(chl_abs):
        high, low_part = halves(chl_abs)
        above = half_dot(jnp.concatenate([high, low_part], axis=1), upper)
        tall = jnp.concatenate([level] * (chl_abs.shape[0] // Y), axis=0)
        return jnp.exp(tall - CHL_ATT / wide * above)

    done = set()
    passed = {}
    outer_rows = []

    def arrive(i):
        if ("x", i) in done:
            return
        done.add(("x", i))
        with jax.named_scope(f"x{i}"):
            crossing[i].wait_recv()
        u, k = ranges[i]
        some = pl.ds(P(u, k), k)
        if i == 0:
            outer.append(remote(raw.at[other, some, body], raw.at[other, past, body], beside))
        passed[i] = beside_rows(other, some)

    def arrive_outer():
        if "outer" in done:
            return
        done.add("outer")
        for i, copy in enumerate(outer):
            with jax.named_scope(f"outer{i}"):
                copy.wait_recv()
        outer_rows.extend(beside_rows(slice(None), pl.ds(P(half, STEPS), STEPS)))

    def ready(first, last):
        if "rows" not in done:
            done.add("rows")
            for i, copy in enumerate(rows):
                with jax.named_scope(f"rows{i}"):
                    copy.wait_recv()
        for i, (u, k) in enumerate(ranges):
            if u <= last and first < u + k:
                arrive(i)
                if ("y", i) not in done:
                    done.add(("y", i))
                    with jax.named_scope(f"passed{i}"):
                        for copy in passed[i]:
                            copy.wait_recv()
        if last >= half:
            arrive_outer()
            if "corner" not in done:
                done.add("corner")
                with jax.named_scope("corner"):
                    for copy in outer_rows:
                        copy.wait_recv()

    windows = [
        (base - STEPS + 1, base + Y + STEPS - 1 - Y),
        (base - 1, base + 1),
        (base,),
    ]

    def stencil(step, p, r):
        here = pl.ds(r, Y)
        up_rows, down_rows = pl.ds(r + 1, Y), pl.ds(r - 1, Y)
        if step == 0:
            wet = raw[wet_field, p, here, :]
            south_wet = raw[wet_field, p, down_rows, :]
            east = raw[fields, p, here, :] * wet * raw[wet_field, p + 1, here, :]
            west = raw[fields, p - 1, here, :] * raw[wet_field, p - 1, here, :] * wet
            up = raw[fields + 1, p, here, :] * wet * raw[wet_field, p, up_rows, :]
            down = raw[fields + 1, p, down_rows, :] * south_wet * wet
            scaled = TIME_STEP * wet
            c = [
                wet
                - scaled
                * (
                    jnp.maximum(east, 0.0) - jnp.minimum(west, 0.0)
                    + jnp.maximum(up, 0.0) - jnp.minimum(down, 0.0)
                ),
                -scaled * jnp.minimum(east, 0.0),
                scaled * jnp.maximum(west, 0.0),
                -scaled * jnp.minimum(up, 0.0),
                scaled * jnp.maximum(down, 0.0),
                scaled,
            ]
            for i, v in enumerate(c):
                coef[i, p, here, :] = v
        else:
            c = [coef[i, p, here, :] for i in range(6)]
        some = pl.ds(0, fields)
        moved = (
            c[0] * state[step, some, p, here, :]
            + c[1] * state[step, some, p + 1, here, :]
            + c[2] * state[step, some, p - 1, here, :]
            + c[3] * state[step, some, p, up_rows, :]
            + c[4] * state[step, some, p, down_rows, :]
        )
        return moved, c[5]

    def advance(*work):
        for step, u, k in work:
            if step == 0:
                ready(u - 1, u + k)
        with jax.named_scope("go" + "_".join(f"{s}:{u}:{k}" for s, u, k in work)):
            compute(work)

    def compute(work):
        tiles = []
        for step, u, k in work:
            p = P(u, k)
            for i in range(k):
                for r in windows[step]:
                    tiles.append((step, p + i, r))
        columns, heats, scales = [], [], []
        for step, p, r in tiles:
            moved, scaled = stencil(step, p, r)
            columns.append(moved[:tracers].reshape(tracers * Y, wide))
            heats.append(moved[tracers])
            scales.append(scaled)
        n = len(tiles)
        mixed = jnp.concatenate(columns, axis=1)
        ahead = half_dot(powers, tall_halves(mixed))
        block = 3 * Y
        result = ahead[3 * block :]

        def part_of(rows, i):
            return stack(rows[i * Y : (i + 1) * Y], wide)

        def spread(v, i):
            return jnp.concatenate([v[i * Y : (i + 1) * Y]] * n, axis=0)

        rates = []
        for sub in range(SUB):
            rows = mixed[:block] if sub == 0 else ahead[(sub - 1) * block : sub * block]
            value = []
            for i in range(3):
                v = part_of(rows, i)
                for j, rate in enumerate(rates):
                    v = v + spread(source[sub - 1 - j], i) * rate
                value.append(v)
            nutrient, chl, phyto = value
            rates.append(
                light(jnp.abs(chl)) * (nutrient / (jnp.abs(nutrient) + HALF_SAT) * phyto)
            )
        chl = part_of(result, 1)
        for j, rate in enumerate(rates):
            chl = chl + spread(source[SUB - 1 - j], 1) * rate
        chl_abs = jnp.abs(chl)
        flat = jnp.concatenate([unstack(rate, Y) for rate in rates], axis=0)
        result = result + half_dot(inject, tall_halves(flat))
        heat = jnp.concatenate(heats, axis=0) + HEAT_GAIN * (
            jnp.concatenate(scales, axis=0) * chl_abs * light(chl_abs)
        )
        for i, (step, p, r) in enumerate(tiles):
            value = result[:, i * wide : (i + 1) * wide].reshape(tracers, Y, wide)
            if step < STEPS - 1:
                here = pl.ds(r, Y)
                state[step + 1, pl.ds(0, tracers), p, here, :] = value
                state[step + 1, tracers, p, here, :] = heat[i * Y : (i + 1) * Y]
            else:
                final[pl.ds(0, tracers), p, :, :] = value
                final[tracers, p, :, :] = heat[i * Y : (i + 1) * Y]

    def leave(u, k):
        some, place = pl.ds(P(u, k), k), pl.ds(B(u, k), k)
        if u >= SHARE:
            remote(final.at[other, some], tracers_out.at[:, place], across)
            arrivals.append(sent[-1])
            remote(final.at[tracers, some], heat_out.at[place], across)
            arrivals.append(sent[-1])
        leaving.append(local(final.at[mine, some], tracers_out.at[:, place]))
        leaving.append(local(final.at[tracers, some], heat_out.at[place]))

    for action in SCHEDULE(half):
        if action[0] == "x":
            arrive(action[1])
        elif action[0] == "z":
            arrive_outer()
        elif action[0] == "go":
            advance(*action[1:])
        else:
            leave(*action[1:])
    with jax.named_scope("leaving"):
        for copy in leaving:
            copy.wait()
    for i, copy in enumerate(arrivals):
        with jax.named_scope(f"arrivals{i}"):
            copy.wait_recv()
    for copy in sent:
        copy.wait_send()


def SCHEDULE(half):
    count = len(pair_plan(half)[1])
    a = FIRST
    b = half - STEPS
    first = [("x", i) for i in range(count)]
    return first + [
        ("go", (0, -2, a + 4)),
        ("go", (1, -1, a + 2)),
        ("go", (2, 0, a)),
        ("out", 0, a),
        ("z",),
        ("go", (0, a + 2, b - a)),
        ("go", (1, a + 1, b - a)),
        ("go", (2, a, b - a)),
        ("out", a, b - a),
        ("go", (0, b + 2, 3)),
        ("go", (1, b + 1, 3)),
        ("go", (2, b, 3)),
        ("out", b, 3),
    ]


def paired(shape, groups, regions, sects):
    return (
        groups == 2 and regions > 1 and regions % 2 == 0 and sects > 1
        and shape[2] == 8 and shape[3] == 128 and shape[1] % 2 == 0 and shape[1] >= 24
        and shape[0] * groups * shape[2] == 128
    )


def pair_call(solute, thermal, eastward, northward, layers, rates, yields, regions, sects):
    own, X, Y, wide = solute.shape
    tracers = own * 2
    half = X // 2
    low, ranges = pair_plan(half)
    columns = half - low + STEPS
    operands = [
        pltpu.with_memory_space_constraint(v, pltpu.HBM)
        for v in (solute, thermal, eastward, northward, layers.T, rates, yields.reshape(1, tracers))
    ]
    hbm = pl.BlockSpec(memory_space=pltpu.HBM)
    free = pl.BlockSpec(memory_space=pl.ANY)
    dma = pltpu.SemaphoreType.DMA
    return pl.pallas_call(
        functools.partial(pair_kernel, regions, sects),
        out_shape=(
            jax.ShapeDtypeStruct(solute.shape, jnp.float32),
            jax.ShapeDtypeStruct(thermal.shape, jnp.float32),
        ),
        in_specs=[hbm] * 7,
        out_specs=(free, free),
        scratch_shapes=[
            pltpu.VMEM((Y, X), jnp.int32),
            pltpu.VMEM((tracers, tracers), jnp.float32),
            pltpu.VMEM((1, tracers), jnp.float32),
            pltpu.VMEM((STEPS, tracers + 4, columns, 2 * Y, wide), jnp.float32),
            pltpu.VMEM((6, columns, 2 * Y, wide), jnp.float32),
            pltpu.VMEM((X, Y, wide), jnp.float32),
            pltpu.VMEM((tracers + 1, columns, Y, wide), jnp.float32),
            dma((SENDS,)),
            dma((SENDS,)),
            dma((LOCALS,)),
        ],
        compiler_params=pltpu.CompilerParams(
            collective_id=0, has_side_effects=True, vmem_limit_bytes=40 << 20
        ),
    )(*operands)


SENDS = 64
LOCALS = 32


def solution(mesh):
    regions, groups, sects = (mesh.shape[a] for a in ("region", "tracer", "sect"))

    def body(solute, thermal, eastward, northward, layers, rates, yields):
        if paired(solute.shape, groups, regions, sects):
            return pair_call(
                solute, thermal, eastward, northward, layers, rates, yields, regions, sects
            )
        own, rows, cols, wide = solute.shape
        tracers = own * groups
        span = rows // groups
        fields = tracers + 1
        flat = (rows * cols, wide)
        free, hbm = pl.BlockSpec(memory_space=pl.ANY), pl.BlockSpec(memory_space=pltpu.HBM)
        dma = pltpu.SemaphoreType.DMA
        peers = max(groups - 1, 1)
        chunks = plan(span)[0]
        mixture, heat = pl.pallas_call(
            functools.partial(kernel, regions, groups, sects),
            out_shape=(
                jax.ShapeDtypeStruct((own, *flat), jnp.float32),
                jax.ShapeDtypeStruct(flat, jnp.float32),
            ),
            in_specs=[hbm] * 7,
            out_specs=(free, free),
            scratch_shapes=[
                pltpu.VMEM((cols, rows), jnp.int32),
                pltpu.VMEM((tracers, tracers), jnp.float32),
                pltpu.VMEM((1, tracers), jnp.float32),
                pltpu.VMEM((STEPS, fields + 3, (span + 2) * cols, wide), jnp.float32),
                pltpu.VMEM((STEPS, chunks, 2, fields + 3, span // chunks, wide), jnp.float32),
                pltpu.VMEM((STEPS, chunks, 2, fields + 3, span // chunks, wide), jnp.float32),
                pltpu.VMEM((6, *flat), jnp.float32),
                pltpu.VMEM((fields, span * cols, wide), jnp.float32),
                dma((peers, chunks)),
                dma((peers, chunks)),
                dma((STEPS, chunks, 4)),
                dma((STEPS, chunks, 4)),
                dma((peers, chunks, 2)),
                dma((peers, chunks, 2)),
                dma((chunks, 3)),
                dma((6,)),
            ],
            compiler_params=pltpu.CompilerParams(
                collective_id=0, has_side_effects=True, vmem_limit_bytes=60 << 20
            ),
        )(
            solute.reshape(own, *flat),
            thermal.reshape(flat),
            eastward.reshape(flat),
            northward.reshape(flat),
            layers.T,
            rates,
            yields.reshape(1, tracers),
        )
        return mixture.reshape(solute.shape), heat.reshape(thermal.shape)

    return jax.shard_map(
        body,
        mesh=mesh,
        in_specs=(
            P("tracer", "region", "sect", None),
            P("region", "sect", None),
            P("region", "sect", None),
            P("region", "sect", None),
            P("region", "sect"),
            P(),
            P(),
        ),
        out_specs=(P("tracer", "region", "sect", None), P("region", "sect", None)),
        check_vma=False,
    )
```

profile of v0, /device:TPU:0, one launch (start us, length us, event | category | flops | bytes accessed | tf_op | source)
XLA Modules:
  0.0 37.4 jit_solution(4926733569607379076)
XLA Ops:
  0.6 35.3 %shard_map.86 = (f32[8,24,8,128]{3,2,1,0:T(8,128)S(1)}, f32[24,8,128]{2,1,0:T(8,128)S(1)}) custom-call(f32[8,24,8,128]{3,2,1,0:T(8,128)} %solute.1, f32[24,8,128]{2,1,0:T(8,128)} %heat_hbm.1, f32[24,8,128]{2,1,0:T(8,128)} %east_hbm.1, f32[24,8,128]{2,1,0:T(8,128)} %north_hbm.1, s32[8,24]{1,0:T(8,128)} %bitcast.2, f32[16,16]{1,0:T(8,128)} %rates_hbm.1, ...), custom_call_target="tpu_custom_call" | custom-call | tf_op jit(solution)/shard_map/pallas_call | solution.py:828
  35.9 0.9 %copy.11 = f32[8,24,8,128]{3,2,1,0:T(8,128)} copy(f32[8,24,8,128]{3,2,1,0:T(8,128)S(1)} %get-tuple-element.4) | data formatting | bytes 1572864
  36.8 0.6 %copy.12 = f32[24,8,128]{2,1,0:T(8,128)} copy(f32[24,8,128]{2,1,0:T(8,128)S(1)} %get-tuple-element.5) | data formatting | bytes 196608
where the time goes:
time: 37.6 us; the launch traced here: 37.4 us
  Pallas kernels  35.3 us (94%)
  local copies, waits for them, and re-layouts  1.52 us (4%)
  between operations  0.64 us (2%)
    pallas_call x1, Pallas kernels, pair_call(): pl.pallas_call(functools.partial(pair_kernel, regions, sects), out_shape=...  35.3 us
    unnamed x2, local copies, waits for them, and re-layouts  1.52 us

commit v1 on v0

--- a/solution.py
+++ b/solution.py
@@ -1,4 +1,5 @@
 import functools
+import math
 
 import jax
 import jax.numpy as jnp
@@ -381,7 +382,7 @@
     for copy in sent + list(arriving.values()):
         copy.wait_send()
 
-SHARE = 0
+SHARE = 3
 FIRST = 3
 
 
@@ -427,13 +428,12 @@
 
 def pair_plan(half):
     low = -SHARE - STEPS
-    ranges, at = [(half - STEPS, STEPS)], SHARE - STEPS
-    while at < half - STEPS:
-        size = min(STEPS, half - STEPS - at)
-        ranges.append((at, size))
-        at += size
-    if SHARE:
-        ranges.append((low, SHARE * 2))
+    ranges = [(half - STEPS, STEPS)]
+    for at, end in ((SHARE - STEPS, half - STEPS), (low, SHARE - STEPS)):
+        while at < end:
+            size = min(STEPS, end - at)
+            ranges.append((at, size))
+            at += size
     return low, ranges
 
 
@@ -441,8 +441,8 @@
     regions, sects,
     solute, heat_hbm, east_hbm, north_hbm, layers_hbm, rates_hbm, yields_hbm,
     tracers_out, heat_out,
-    layers_in, rates_ref, yields_ref, state, coef, wets, final,
-    send_sem, recv_sem, local_sem,
+    layers_in, rates_ref, yields_ref, state, coef, wets, final, measure,
+    send_sem, recv_sem,
 ):
     groups = 2
     region, group, sect = (lax.axis_index(a) for a in ("region", "tracer", "sect"))
@@ -475,53 +475,72 @@
     across = {"tracer": peer}
     mine, other = pl.ds(group * own, own), pl.ds(peer * own, own)
 
+    names, lines = {}, {}
+
+    def slot(name):
+        return names.setdefault(name, len(names))
+
+    def tally(name, ref):
+        lines[name] = lines.get(name, 0) + math.prod(ref.shape) // wide
+
+    def settle(name, sems=recv_sem):
+        some = measure.at[pl.ds(0, lines[name])]
+        at = slot(name) if sems is recv_sem else int(name[4:])
+        with jax.named_scope(name):
+            pltpu.make_async_copy(some, some, sems.at[at]).wait()
+
+    def local(name, source_ref, target_ref):
+        tally(name, target_ref)
+        pltpu.make_async_copy(source_ref, target_ref, recv_sem.at[slot(name)]).start()
+
+    def remote(name, source_ref, target_ref, device, turn=0):
+        tally(name, target_ref)
+        tally(f"sent{turn}", source_ref)
+        push(name, source_ref, target_ref, device, turn)
+
+    def push(name, source_ref, target_ref, device, turn=0):
+        pltpu.make_async_remote_copy(
+            src_ref=source_ref,
+            dst_ref=target_ref,
+            send_sem=send_sem.at[turn],
+            recv_sem=recv_sem.at[slot(name)],
+            device_id=device,
+            device_id_type=MESH,
+        ).start()
+
+    raw = state.at[0]
+    body = pl.ds(base, Y)
+    blank = jnp.zeros((tracers + 4, 1, STEPS, wide), jnp.float32)
+    for u in (low, half, half + 1, half + 2):
+        for row in (base - STEPS, base + Y):
+            raw[:, pl.ds(P(u, 1), 1), pl.ds(row, STEPS), :] = blank
     barrier = pltpu.get_barrier_semaphore()
     for device in (across, beside, north, south):
         pl.semaphore_signal(barrier, inc=1, device_id=device, device_id_type=MESH)
 
-    count = [0, 0]
-    sent, leaving, arrivals = [], [], []
-
-    def local(source_ref, target_ref):
-        copy = pltpu.make_async_copy(source_ref, target_ref, local_sem.at[count[0]])
-        count[0] += 1
+    small = [
+        pltpu.make_async_copy(source_ref, target_ref, recv_sem.at[slot(f"small{i}")])
+        for i, (source_ref, target_ref) in enumerate(
+            ((layers_hbm, layers_in), (rates_hbm, rates_ref), (yields_hbm, yields_ref))
+        )
+    ]
+    for copy in small:
         copy.start()
-        return copy
-
-    def remote(source_ref, target_ref, device):
-        copy = pltpu.make_async_remote_copy(
-            src_ref=source_ref,
-            dst_ref=target_ref,
-            send_sem=send_sem.at[count[1]],
-            recv_sem=recv_sem.at[count[1]],
-            device_id=device,
-            device_id_type=MESH,
-        )
-        count[1] += 1
-        copy.start()
-        sent.append(copy)
-        return copy
-
-    raw = state.at[0]
-    body = pl.ds(base, Y)
-    tables_in = [
-        local(layers_hbm, layers_in),
-        local(rates_hbm, rates_ref),
-        local(yields_hbm, yields_ref),
-    ]
     p_all, b_all = P(low, reach), B(low, reach)
     in_block = pl.ds(b_all, reach)
     in_state = pl.ds(p_all, reach)
     extra = ((heat_hbm, tracers), (east_hbm, fields), (north_hbm, fields + 1))
-    loads = [local(solute.at[:, in_block], raw.at[mine, in_state, body])]
+    local("loads", solute.at[:, in_block], raw.at[mine, in_state, body])
     for ref, field in extra:
-        loads.append(local(ref.at[in_block], raw.at[field, in_state, body]))
-
-    with jax.named_scope('barrier'):
+        local("loads", ref.at[in_block], raw.at[field, in_state, body])
+
+    with jax.named_scope("barrier"):
         pl.semaphore_wait(barrier, 4)
 
-    def cross(u, k):
-        return remote(
+    def cross(i):
+        u, k = ranges[i]
+        remote(
+            f"x{i}",
             solute.at[:, pl.ds(B(u, k, 1 - part), k)],
             raw.at[mine, pl.ds(P(u, k, 1 - part), k), body],
             across,
@@ -531,38 +550,65 @@
     edge_block = pl.ds(B(edge, STEPS), STEPS)
     edge_state = pl.ds(P(edge, STEPS), STEPS)
     past = pl.ds(pick(part, reach, 0), STEPS)
-    crossing = [cross(*ranges[0])]
-    outer = [remote(solute.at[:, edge_block], raw.at[mine, past, body], beside)]
+    cross(0)
+    remote("outer", solute.at[:, edge_block], raw.at[mine, past, body], beside)
     for ref, field in extra:
-        outer.append(remote(ref.at[edge_block], raw.at[field, past, body], beside))
-    crossing += [cross(*r) for r in ranges[1:]]
-    sides = (
-        (pl.ds(Y - STEPS, STEPS), pl.ds(base - STEPS, STEPS), north),
-        (pl.ds(0, STEPS), pl.ds(base + Y, STEPS), south),
-    )
-    rows = []
-    for block_rows, halo_rows, device in sides:
-        rows.append(
-            remote(
-                solute.at[:, in_block, block_rows], raw.at[mine, in_state, halo_rows], device
-            )
-        )
-        for ref, field in extra:
-            rows.append(
-                remote(ref.at[in_block, block_rows], raw.at[field, in_state, halo_rows], device)
-            )
-
-    def beside_rows(some, place):
-        return [
-            remote(
-                raw.at[some, place, pl.ds(base + y, STEPS)],
-                raw.at[some, place, halo_rows],
+        remote("outer", ref.at[edge_block], raw.at[field, past, body], beside)
+    for i in range(1, len(ranges)):
+        cross(i)
+    far = sect % 2
+
+    def both_sides(send):
+        for first in (0, 1):
+            @pl.when(far == first)
+            def _():
+                for side in (first, 1 - first):
+                    send(side, (south, north)[side])
+
+    def halo_row(side, deep=STEPS):
+        return pl.ds(base - deep if side else base + Y, deep)
+
+    def tally_sides(name, refs):
+        for ref in refs:
+            for _ in range(2):
+                tally(name, ref)
+                tally("sent0", ref)
+
+    def direct_rows(name, u, k):
+        b, p = pl.ds(B(u, k), k), pl.ds(P(u, k), k)
+        refs = [(solute.at[:, b], mine)] + [(ref.at[b], field) for ref, field in extra]
+
+        def send(side, device):
+            block_rows = pl.ds(Y - STEPS if side else 0, STEPS)
+            for ref, field in refs:
+                rows = ref.at[:, :, block_rows] if ref is refs[0][0] else ref.at[:, block_rows]
+                push(name, rows, raw.at[field, p, halo_row(side)], device)
+
+        both_sides(send)
+        tally_sides(name, [raw.at[field, p, halo_row(0)] for _, field in refs])
+
+    def beside_rows(name, some, u, k, deep=STEPS):
+        place = pl.ds(P(u, k), k)
+
+        def send(side, device):
+            start = base + Y - deep if side else base
+            push(
+                name,
+                raw.at[some, place, pl.ds(start, deep)],
+                raw.at[some, place, halo_row(side, deep)],
                 device,
             )
-            for y, (_, halo_rows, device) in zip((Y - STEPS, 0), sides)
-        ]
-
-    for copy in tables_in:
+
+        both_sides(send)
+        tally_sides(name, [raw.at[some, place, halo_row(0, deep)]])
+
+    near = 1 + -(-(FIRST + 2 * STEPS) // STEPS)
+    cone = min((near - 1) * STEPS, edge + STEPS + STEPS - SHARE)
+    cone_at = max(low + 1, SHARE - STEPS)
+    cone_end = SHARE - STEPS + cone
+    direct_rows("rows", cone_at, cone_end - cone_at)
+
+    for copy in small:
         copy.wait()
     total = X * Y
     pick_rows = iota((total, X), 0) // Y == iota((total, X), 1)
@@ -579,18 +625,17 @@
     )
     wet_field = fields + 2
     raw[wet_field, in_state, body, :] = wets[in_block]
-    outer.append(remote(raw.at[wet_field, edge_state, body], raw.at[wet_field, past, body], beside))
-    rows += beside_rows(wet_field, in_state)
-
-    with jax.named_scope('tables'):
+    remote("outer", raw.at[wet_field, edge_state, body], raw.at[wet_field, past, body], beside)
+    beside_rows("rows", pl.ds(wet_field, 1), low + 1, reach - 1)
+
+    with jax.named_scope("make_tables"):
         powers, inject, source = pair_tables(rates_ref, yields_ref, tracers, wide, Y)
     shape = (wide, wide)
     upper = (iota(shape, 0) < iota(shape, 1)).astype(jnp.float32)
     upper = upper + 0.5 * (iota(shape, 0) == iota(shape, 1)).astype(jnp.float32)
     upper = jnp.concatenate([upper.astype(jnp.bfloat16)] * 2, axis=0)
     level = (iota((Y, wide), 1).astype(jnp.float32) + 0.5) * (-WATER_ATT / wide)
-    for copy in loads:
-        copy.wait()
+    settle("loads")
 
     def light(chl_abs):
         high, low_part = halves(chl_abs)
@@ -599,51 +644,47 @@
         return jnp.exp(tall - CHL_ATT / wide * above)
 
     done = set()
-    passed = {}
-    outer_rows = []
+
+    def once(name):
+        fresh = name not in done
+        done.add(name)
+        return fresh
 
     def arrive(i):
-        if ("x", i) in done:
-            return
-        done.add(("x", i))
-        with jax.named_scope(f"x{i}"):
-            crossing[i].wait_recv()
-        u, k = ranges[i]
-        some = pl.ds(P(u, k), k)
-        if i == 0:
-            outer.append(remote(raw.at[other, some, body], raw.at[other, past, body], beside))
-        passed[i] = beside_rows(other, some)
+        if once(f"x{i}"):
+            settle(f"x{i}")
+            u, k = ranges[i]
+            some = pl.ds(P(u, k), k)
+            if i == 0:
+                remote("outer", raw.at[other, some, body], raw.at[other, past, body], beside)
+            skip = int(u == low)
+            beside_rows(f"y{i}", other, u + skip, k - skip)
+            if i == near - 1:
+                if cone_end < half:
+                    direct_rows("rest", cone_end, half - cone_end)
+                if low + 1 < cone_at:
+                    direct_rows("rest", low + 1, cone_at - low - 1)
 
     def arrive_outer():
-        if "outer" in done:
-            return
-        done.add("outer")
-        for i, copy in enumerate(outer):
-            with jax.named_scope(f"outer{i}"):
-                copy.wait_recv()
-        outer_rows.extend(beside_rows(slice(None), pl.ds(P(half, STEPS), STEPS)))
+        arrive(0)
+        if once("outer"):
+            settle("outer")
+            beside_rows("corner", slice(None), half, STEPS - 1, STEPS - 1)
 
     def ready(first, last):
-        if "rows" not in done:
-            done.add("rows")
-            for i, copy in enumerate(rows):
-                with jax.named_scope(f"rows{i}"):
-                    copy.wait_recv()
+        if once("rows"):
+            settle("rows")
+        if (first < cone_at - 1 or last >= cone_end) and "rest" in lines and once("rest"):
+            settle("rest")
         for i, (u, k) in enumerate(ranges):
             if u <= last and first < u + k:
                 arrive(i)
-                if ("y", i) not in done:
-                    done.add(("y", i))
-                    with jax.named_scope(f"passed{i}"):
-                        for copy in passed[i]:
-                            copy.wait_recv()
+                if once(f"y{i}"):
+                    settle(f"y{i}")
         if last >= half:
             arrive_outer()
-            if "corner" not in done:
-                done.add("corner")
-                with jax.named_scope("corner"):
-                    for copy in outer_rows:
-                        copy.wait_recv()
+            if once("corner"):
+                settle("corner")
 
     windows = [
         (base - STEPS + 1, base + Y + STEPS - 1 - Y),
@@ -756,14 +797,12 @@
     def leave(u, k):
         some, place = pl.ds(P(u, k), k), pl.ds(B(u, k), k)
         if u >= SHARE:
-            remote(final.at[other, some], tracers_out.at[:, place], across)
-            arrivals.append(sent[-1])
-            remote(final.at[tracers, some], heat_out.at[place], across)
-            arrivals.append(sent[-1])
-        leaving.append(local(final.at[mine, some], tracers_out.at[:, place]))
-        leaving.append(local(final.at[tracers, some], heat_out.at[place]))
-
-    for action in SCHEDULE(half):
+            remote("arrivals", final.at[other, some], tracers_out.at[:, place], across, 1)
+            remote("arrivals", final.at[tracers, some], heat_out.at[place], across, 1)
+        local("leaving", final.at[mine, some], tracers_out.at[:, place])
+        local("leaving", final.at[tracers, some], heat_out.at[place])
+
+    for action in schedule(half):
         if action[0] == "x":
             arrive(action[1])
         elif action[0] == "z":
@@ -772,36 +811,32 @@
             advance(*action[1:])
         else:
             leave(*action[1:])
-    with jax.named_scope("leaving"):
-        for copy in leaving:
-            copy.wait()
-    for i, copy in enumerate(arrivals):
-        with jax.named_scope(f"arrivals{i}"):
-            copy.wait_recv()
-    for copy in sent:
-        copy.wait_send()
-
-
-def SCHEDULE(half):
+    settle("leaving")
+    settle("arrivals")
+    settle("sent0", send_sem)
+    settle("sent1", send_sem)
+
+
+def schedule(half):
     count = len(pair_plan(half)[1])
-    a = FIRST
-    b = half - STEPS
-    first = [("x", i) for i in range(count)]
-    return first + [
-        ("go", (0, -2, a + 4)),
-        ("go", (1, -1, a + 2)),
-        ("go", (2, 0, a)),
-        ("out", 0, a),
-        ("z",),
-        ("go", (0, a + 2, b - a)),
-        ("go", (1, a + 1, b - a)),
-        ("go", (2, a, b - a)),
-        ("out", a, b - a),
-        ("go", (0, b + 2, 3)),
-        ("go", (1, b + 1, 3)),
-        ("go", (2, b, 3)),
-        ("out", b, 3),
+    h, a, b = SHARE, FIRST, half - STEPS
+    near = 1 + -(-(a + 2 * STEPS) // STEPS)
+    inner = [[(s, -h - 2 + s, 2 * h)] if h else [] for s in range(STEPS)]
+    own = 1 + -(-(b - h + STEPS) // STEPS)
+    rest = half - h - a
+    plan = [("x", i) for i in range(own)]
+    plan += [("z",), ("go", (0, h - 2, a + 4)), ("go", (1, h - 1, a + 2))]
+    plan += [("x", i) for i in range(own, count)]
+    plan += [
+        ("go", (2, h, a), (0, h + a + 2, rest)),
+        ("out", h, a),
+        ("go", (1, h + a + 1, rest)),
+        ("go", (2, h + a, rest)),
+        ("out", h + a, rest),
     ]
+    for s in range(STEPS if h else 0):
+        plan.append(("go", *inner[s]))
+    return plan + ([("out", -h, 2 * h)] if h else [])
 
 
 def paired(shape, groups, regions, sects):
@@ -841,9 +876,9 @@
             pltpu.VMEM((6, columns, 2 * Y, wide), jnp.float32),
             pltpu.VMEM((X, Y, wide), jnp.float32),
             pltpu.VMEM((tracers + 1, columns, Y, wide), jnp.float32),
-            dma((SENDS,)),
-            dma((SENDS,)),
-            dma((LOCALS,)),
+            pltpu.VMEM((MEASURE, wide), jnp.float32),
+            dma((2,)),
+            dma((len(ranges) * 2 + 10,)),
         ],
         compiler_params=pltpu.CompilerParams(
             collective_id=0, has_side_effects=True, vmem_limit_bytes=40 << 20
@@ -851,8 +886,7 @@
     )(*operands)
 
 
-SENDS = 64
-LOCALS = 32
+MEASURE = 8192
 
 
 def solution(mesh):

time: 37.6 us -> 33.4 us (0.89); the launches traced: 37.4 us -> 32.8 us
  Pallas kernels: 35.3 us -> 30.7 us
    pallas_call x1, Pallas kernels: 35.3 us -> 30.7 us  [pair_call(): pl.pallas_call(functools.partial(pair_kernel, regions, sects), out_shape=...]
where the time goes in v1:
time: 33.4 us; the launch traced here: 32.8 us
  Pallas kernels  30.7 us (92%)
  local copies, waits for them, and re-layouts  1.52 us (5%)
  between operations  0.64 us (2%)
    pallas_call x1, Pallas kernels, pair_call(): pl.pallas_call(functools.partial(pair_kernel, regions, sects), out_shape=...  30.7 us
    unnamed x2, local copies, waits for them, and re-layouts  1.52 us

profile of v1, /device:TPU:0, one launch (start us, length us, event | category | flops | bytes accessed | tf_op | source)
XLA Modules:
  0.0 32.8 jit_solution(5702237769610739738)
XLA Ops:
  0.6 30.7 %shard_map.86 = (f32[8,24,8,128]{3,2,1,0:T(8,128)S(1)}, f32[24,8,128]{2,1,0:T(8,128)S(1)}) custom-call(f32[8,24,8,128]{3,2,1,0:T(8,128)} %solute.1, f32[24,8,128]{2,1,0:T(8,128)} %heat_hbm.1, f32[24,8,128]{2,1,0:T(8,128)} %east_hbm.1, f32[24,8,128]{2,1,0:T(8,128)} %north_hbm.1, s32[8,24]{1,0:T(8,128)} %bitcast.2, f32[16,16]{1,0:T(8,128)} %rates_hbm.1, ...), custom_call_target="tpu_custom_call" | custom-call | tf_op jit(solution)/shard_map/pallas_call | solution.py:863
  31.3 0.9 %copy.11 = f32[8,24,8,128]{3,2,1,0:T(8,128)} copy(f32[8,24,8,128]{3,2,1,0:T(8,128)S(1)} %get-tuple-element.4) | data formatting | bytes 1572864
  32.2 0.6 %copy.12 = f32[24,8,128]{2,1,0:T(8,128)} copy(f32[24,8,128]{2,1,0:T(8,128)S(1)} %get-tuple-element.5) | data formatting | bytes 196608

commit v2 on v1

--- a/solution.py
+++ b/solution.py
@@ -382,7 +382,7 @@
     for copy in sent + list(arriving.values()):
         copy.wait_send()
 
-SHARE = 3
+SHARE = 5
 FIRST = 3
 
 
@@ -607,6 +607,10 @@
     cone_at = max(low + 1, SHARE - STEPS)
     cone_end = SHARE - STEPS + cone
     direct_rows("rows", cone_at, cone_end - cone_at)
+    if cone_end < half:
+        direct_rows("rest", cone_end, half - cone_end)
+    if low + 1 < cone_at:
+        direct_rows("rest", low + 1, cone_at - low - 1)
 
     for copy in small:
         copy.wait()
@@ -659,11 +663,6 @@
                 remote("outer", raw.at[other, some, body], raw.at[other, past, body], beside)
             skip = int(u == low)
             beside_rows(f"y{i}", other, u + skip, k - skip)
-            if i == near - 1:
-                if cone_end < half:
-                    direct_rows("rest", cone_end, half - cone_end)
-                if low + 1 < cone_at:
-                    direct_rows("rest", low + 1, cone_at - low - 1)
 
     def arrive_outer():
         arrive(0)
@@ -731,6 +730,7 @@
         return moved, c[5]
 
     def advance(*work):
+        work = [item for item in work if item[2] > 0]
         for step, u, k in work:
             if step == 0:
                 ready(u - 1, u + k)
@@ -795,6 +795,8 @@
                 final[tracers, p, :, :] = heat[i * Y : (i + 1) * Y]
 
     def leave(u, k):
+        if k <= 0:
+            return
         some, place = pl.ds(P(u, k), k), pl.ds(B(u, k), k)
         if u >= SHARE:
             remote("arrivals", final.at[other, some], tracers_out.at[:, place], across, 1)
@@ -823,17 +825,14 @@
     near = 1 + -(-(a + 2 * STEPS) // STEPS)
     inner = [[(s, -h - 2 + s, 2 * h)] if h else [] for s in range(STEPS)]
     own = 1 + -(-(b - h + STEPS) // STEPS)
-    rest = half - h - a
+    rest = b - h - a
+    late = [("x", i) for i in range(own, count)]
     plan = [("x", i) for i in range(own)]
-    plan += [("z",), ("go", (0, h - 2, a + 4)), ("go", (1, h - 1, a + 2))]
-    plan += [("x", i) for i in range(own, count)]
-    plan += [
-        ("go", (2, h, a), (0, h + a + 2, rest)),
-        ("out", h, a),
-        ("go", (1, h + a + 1, rest)),
-        ("go", (2, h + a, rest)),
-        ("out", h + a, rest),
-    ]
+    plan += [("go", (0, h - 2, a + 4)), ("z",), *late[:1], ("go", (1, h - 1, a + 2)), *late[1:2]]
+    plan += [("go", (2, h, a), (0, h + a + 2, rest)), ("out", h, a)]
+    plan += [("go", (1, h + a + 1, rest), (0, b + 2, 3)), *late[2:]]
+    plan += [("go", (2, h + a, rest), (1, b + 1, 3)), ("out", h + a, rest)]
+    plan += [("go", (2, b, 3)), ("out", b, 3)]
     for s in range(STEPS if h else 0):
         plan.append(("go", *inner[s]))
     return plan + ([("out", -h, 2 * h)] if h else [])
@@ -845,6 +844,18 @@
         and shape[2] == 8 and shape[3] == 128 and shape[1] % 2 == 0 and shape[1] >= 24
         and shape[0] * groups * shape[2] == 128
     )
+
+
+def write_out(mixture, heat, mixture_out, heat_out, sems):
+    own = mixture.shape[0]
+    copies = [
+        pltpu.make_async_copy(mixture.at[i], mixture_out.at[i], sems.at[i]) for i in range(own)
+    ]
+    copies.append(pltpu.make_async_copy(heat, heat_out, sems.at[own]))
+    for copy in copies:
+        copy.start()
+    for copy in copies:
+        copy.wait()
 
 
 def pair_call(solute, thermal, eastward, northward, layers, rates, yields, regions, sects):
@@ -860,7 +871,7 @@
     hbm = pl.BlockSpec(memory_space=pltpu.HBM)
     free = pl.BlockSpec(memory_space=pl.ANY)
     dma = pltpu.SemaphoreType.DMA
-    return pl.pallas_call(
+    mixture, heat = pl.pallas_call(
         functools.partial(pair_kernel, regions, sects),
         out_shape=(
             jax.ShapeDtypeStruct(solute.shape, jnp.float32),
@@ -884,6 +895,17 @@
             collective_id=0, has_side_effects=True, vmem_limit_bytes=40 << 20
         ),
     )(*operands)
+    return pl.pallas_call(
+        write_out,
+        out_shape=(
+            jax.ShapeDtypeStruct(solute.shape, jnp.float32),
+            jax.ShapeDtypeStruct(thermal.shape, jnp.float32),
+        ),
+        in_specs=[free] * 2,
+        out_specs=(hbm, hbm),
+        scratch_shapes=[dma((own + 1,))],
+        compiler_params=pltpu.CompilerParams(vmem_limit_bytes=1 << 20),
+    )(mixture, heat)
 
 
 MEASURE = 8192

time: 33.4 us -> 31.6 us (0.946)
  local copies, waits for them, and re-layouts: 1.52 us -> 0 us
    unnamed x2 -> x0, local copies, waits for them, and re-layouts: 1.52 us -> none
    pallas_call x1, Pallas kernels: 30.7 us -> 29.6 us  [pair_call(): pl.pallas_call(functools.partial(pair_kernel, regions, sects), out_shape=...]
    pallas_call x0 -> x1, Pallas kernels: none -> 0.98 us  [pair_call(): pl.pallas_call(write_out, out_shape=(jax.ShapeDtypeStruct(solute.shape, j...]
where the time goes in v2:
time: 31.6 us; the launch traced here: 31.2 us
  Pallas kernels  30.6 us (97%)
  between operations  0.64 us (2%)
    pallas_call x1, Pallas kernels, pair_call(): pl.pallas_call(functools.partial(pair_kernel, regions, sects), out_shape=...  29.6 us
    pallas_call x1, Pallas kernels, pair_call(): pl.pallas_call(write_out, out_shape=(jax.ShapeDtypeStruct(solute.shape, j...  0.98 us

profile of v2, /device:TPU:0, one launch (start us, length us, event | category | flops | bytes accessed | tf_op | source)
XLA Modules:
  0.0 31.2 jit_solution(7467484789403301327)
XLA Ops:
  0.6 29.6 %shard_map.86 = (f32[8,24,8,128]{3,2,1,0:T(8,128)S(1)}, f32[24,8,128]{2,1,0:T(8,128)S(1)}) custom-call(f32[8,24,8,128]{3,2,1,0:T(8,128)} %solute.1, f32[24,8,128]{2,1,0:T(8,128)} %heat_hbm.1, f32[24,8,128]{2,1,0:T(8,128)} %east_hbm.1, f32[24,8,128]{2,1,0:T(8,128)} %north_hbm.1, s32[8,24]{1,0:T(8,128)} %bitcast.2, f32[16,16]{1,0:T(8,128)} %rates_hbm.1, ...), custom_call_target="tpu_custom_call" | custom-call | tf_op jit(solution)/shard_map/pallas_call | solution.py:874
  30.2 1.0 %shard_map.87 = (f32[8,24,8,128]{3,2,1,0:T(8,128)}, f32[24,8,128]{2,1,0:T(8,128)}) custom-call(f32[8,24,8,128]{3,2,1,0:T(8,128)S(1)} %get-tuple-element.4.mixture, f32[24,8,128]{2,1,0:T(8,128)S(1)} %get-tuple-element.5.heat), custom_call_target="tpu_custom_call" | custom-call | tf_op jit(solution)/shard_map/pallas_call | solution.py:898

commit v3 on v2

--- a/solution.py
+++ b/solution.py
@@ -442,7 +442,7 @@
     solute, heat_hbm, east_hbm, north_hbm, layers_hbm, rates_hbm, yields_hbm,
     tracers_out, heat_out,
     layers_in, rates_ref, yields_ref, state, coef, wets, final, measure,
-    send_sem, recv_sem,
+    send_sem, recv_sem, go_sem,
 ):
     groups = 2
     region, group, sect = (lax.axis_index(a) for a in ("region", "tracer", "sect"))
@@ -515,7 +515,11 @@
         for row in (base - STEPS, base + Y):
             raw[:, pl.ds(P(u, 1), 1), pl.ds(row, STEPS), :] = blank
     barrier = pltpu.get_barrier_semaphore()
-    for device in (across, beside, north, south):
+    @pl.when(part == 0)
+    def _():
+        pl.semaphore_signal(barrier, inc=1, device_id=beside, device_id_type=MESH)
+
+    for device in (across, north, south):
         pl.semaphore_signal(barrier, inc=1, device_id=device, device_id_type=MESH)
 
     small = [
@@ -535,7 +539,7 @@
         local("loads", ref.at[in_block], raw.at[field, in_state, body])
 
     with jax.named_scope("barrier"):
-        pl.semaphore_wait(barrier, 4)
+        pl.semaphore_wait(barrier, 3 + part)
 
     def cross(i):
         u, k = ranges[i]
@@ -551,9 +555,18 @@
     edge_state = pl.ds(P(edge, STEPS), STEPS)
     past = pl.ds(pick(part, reach, 0), STEPS)
     cross(0)
-    remote("outer", solute.at[:, edge_block], raw.at[mine, past, body], beside)
-    for ref, field in extra:
-        remote("outer", ref.at[edge_block], raw.at[field, past, body], beside)
+    edges = [(solute.at[:, edge_block], raw.at[mine, past, body])]
+    edges += [(ref.at[edge_block], raw.at[field, past, body]) for ref, field in extra]
+    for source_ref, target_ref in edges:
+        tally("outer", target_ref)
+        tally("sent0", source_ref)
+
+    @pl.when(part == 1)
+    def _():
+        pl.semaphore_signal(go_sem, inc=1, device_id=beside, device_id_type=MESH)
+        for source_ref, target_ref in edges:
+            push("outer", source_ref, target_ref, beside)
+
     for i in range(1, len(ranges)):
         cross(i)
     far = sect % 2
@@ -609,8 +622,6 @@
     direct_rows("rows", cone_at, cone_end - cone_at)
     if cone_end < half:
         direct_rows("rest", cone_end, half - cone_end)
-    if low + 1 < cone_at:
-        direct_rows("rest", low + 1, cone_at - low - 1)
 
     for copy in small:
         copy.wait()
@@ -629,11 +640,17 @@
     )
     wet_field = fields + 2
     raw[wet_field, in_state, body, :] = wets[in_block]
-    remote("outer", raw.at[wet_field, edge_state, body], raw.at[wet_field, past, body], beside)
     beside_rows("rows", pl.ds(wet_field, 1), low + 1, reach - 1)
 
     with jax.named_scope("make_tables"):
         powers, inject, source = pair_tables(rates_ref, yields_ref, tracers, wide, Y)
+    @pl.when(part == 0)
+    def _():
+        pl.semaphore_wait(go_sem, 1)
+        for source_ref, target_ref in edges:
+            push("outer", source_ref, target_ref, beside)
+
+    remote("outer", raw.at[wet_field, edge_state, body], raw.at[wet_field, past, body], beside)
     shape = (wide, wide)
     upper = (iota(shape, 0) < iota(shape, 1)).astype(jnp.float32)
     upper = upper + 0.5 * (iota(shape, 0) == iota(shape, 1)).astype(jnp.float32)
@@ -663,6 +680,8 @@
                 remote("outer", raw.at[other, some, body], raw.at[other, past, body], beside)
             skip = int(u == low)
             beside_rows(f"y{i}", other, u + skip, k - skip)
+            if i == near - 1 and low + 1 < cone_at:
+                direct_rows("inner", low + 1, cone_at - low - 1)
 
     def arrive_outer():
         arrive(0)
@@ -673,8 +692,9 @@
     def ready(first, last):
         if once("rows"):
             settle("rows")
-        if (first < cone_at - 1 or last >= cone_end) and "rest" in lines and once("rest"):
-            settle("rest")
+        for name, wanted in (("inner", first < cone_at), ("rest", last >= cone_end)):
+            if wanted and name in lines and once(name):
+                settle(name)
         for i, (u, k) in enumerate(ranges):
             if u <= last and first < u + k:
                 arrive(i)
@@ -830,7 +850,7 @@
     plan = [("x", i) for i in range(own)]
     plan += [("go", (0, h - 2, a + 4)), ("z",), *late[:1], ("go", (1, h - 1, a + 2)), *late[1:2]]
     plan += [("go", (2, h, a), (0, h + a + 2, rest)), ("out", h, a)]
-    plan += [("go", (1, h + a + 1, rest), (0, b + 2, 3)), *late[2:]]
+    plan += [*late[2:], ("go", (1, h + a + 1, rest), (0, b + 2, 3))]
     plan += [("go", (2, h + a, rest), (1, b + 1, 3)), ("out", h + a, rest)]
     plan += [("go", (2, b, 3)), ("out", b, 3)]
     for s in range(STEPS if h else 0):
@@ -889,7 +909,8 @@
             pltpu.VMEM((tracers + 1, columns, Y, wide), jnp.float32),
             pltpu.VMEM((MEASURE, wide), jnp.float32),
             dma((2,)),
-            dma((len(ranges) * 2 + 10,)),
+            dma((len(ranges) * 2 + 11,)),
+            pltpu.SemaphoreType.REGULAR,
         ],
         compiler_params=pltpu.CompilerParams(
             collective_id=0, has_side_effects=True, vmem_limit_bytes=40 << 20

time: 31.6 us -> 30 us (0.949)
  Pallas kernels: 30.6 us -> 29.2 us
    pallas_call x1, Pallas kernels: 29.6 us -> 28.2 us  [pair_call(): pl.pallas_call(functools.partial(pair_kernel, regions, sects), out_shape=...]
where the time goes in v3:
time: 30 us; the launch traced here: 29.8 us
  Pallas kernels  29.2 us (97%)
  between operations  0.64 us (2%)
    pallas_call x1, Pallas kernels, pair_call(): pl.pallas_call(functools.partial(pair_kernel, regions, sects), out_shape=...  28.2 us
    pallas_call x1, Pallas kernels, pair_call(): pl.pallas_call(write_out, out_shape=(jax.ShapeDtypeStruct(solute.shape, j...  0.98 us

profile of v3, /device:TPU:0, one launch (start us, length us, event | category | flops | bytes accessed | tf_op | source)
XLA Modules:
  0.0 29.8 jit_solution(17370494839390860091)
XLA Ops:
  0.6 28.2 %shard_map.86 = (f32[8,24,8,128]{3,2,1,0:T(8,128)S(1)}, f32[24,8,128]{2,1,0:T(8,128)S(1)}) custom-call(f32[8,24,8,128]{3,2,1,0:T(8,128)} %solute.1, f32[24,8,128]{2,1,0:T(8,128)} %heat_hbm.1, f32[24,8,128]{2,1,0:T(8,128)} %east_hbm.1, f32[24,8,128]{2,1,0:T(8,128)} %north_hbm.1, s32[8,24]{1,0:T(8,128)} %bitcast.2, f32[16,16]{1,0:T(8,128)} %rates_hbm.1, ...), custom_call_target="tpu_custom_call" | custom-call | tf_op jit(solution)/shard_map/pallas_call | solution.py:894
  28.8 1.0 %shard_map.87 = (f32[8,24,8,128]{3,2,1,0:T(8,128)}, f32[24,8,128]{2,1,0:T(8,128)}) custom-call(f32[8,24,8,128]{3,2,1,0:T(8,128)S(1)} %get-tuple-element.4.mixture, f32[24,8,128]{2,1,0:T(8,128)S(1)} %get-tuple-element.5.heat), custom_call_target="tpu_custom_call" | custom-call | tf_op jit(solution)/shard_map/pallas_call | solution.py:919

commit v4 on v3

--- a/solution.py
+++ b/solution.py
@@ -772,9 +772,14 @@
             scales.append(scaled)
         n = len(tiles)
         mixed = jnp.concatenate(columns, axis=1)
-        ahead = half_dot(powers, tall_halves(mixed))
+        parts = tall_halves(mixed)
         block = 3 * Y
-        result = ahead[3 * block :]
+        if n <= 2 * STEPS:
+            ahead = half_dot(powers[: 3 * block], parts)
+            result = half_dot(powers[3 * block :], parts)
+        else:
+            ahead = half_dot(powers, parts)
+            result = ahead[3 * block :]
 
         def part_of(rows, i):
             return stack(rows[i * Y : (i + 1) * Y], wide)
@@ -867,11 +872,8 @@
 
 
 def write_out(mixture, heat, mixture_out, heat_out, sems):
-    own = mixture.shape[0]
-    copies = [
-        pltpu.make_async_copy(mixture.at[i], mixture_out.at[i], sems.at[i]) for i in range(own)
-    ]
-    copies.append(pltpu.make_async_copy(heat, heat_out, sems.at[own]))
+    copies = [pltpu.make_async_copy(mixture, mixture_out, sems.at[0])]
+    copies.append(pltpu.make_async_copy(heat, heat_out, sems.at[1]))
     for copy in copies:
         copy.start()
     for copy in copies:
@@ -924,7 +926,7 @@
         ),
         in_specs=[free] * 2,
         out_specs=(hbm, hbm),
-        scratch_shapes=[dma((own + 1,))],
+        scratch_shapes=[dma((2,))],
         compiler_params=pltpu.CompilerParams(vmem_limit_bytes=1 << 20),
     )(mixture, heat)
 

time: 30 us -> 29.9 us (level)
  no operation moved by 1% of the time
where the time goes in v4:
time: 29.9 us; the launch traced here: 29.8 us
  Pallas kernels  29.1 us (97%)
  between operations  0.64 us (2%)
    pallas_call x1, Pallas kernels, pair_call(): pl.pallas_call(functools.partial(pair_kernel, regions, sects), out_shape=...  28.2 us
    pallas_call x1, Pallas kernels, pair_call(): pl.pallas_call(write_out, out_shape=(jax.ShapeDtypeStruct(solute.shape, j...  0.92 us

profile of v4, /device:TPU:0, one launch (start us, length us, event | category | flops | bytes accessed | tf_op | source)
XLA Modules:
  0.0 29.8 jit_solution(9421907481634413356)
XLA Ops:
  0.6 28.2 %shard_map.86 = (f32[8,24,8,128]{3,2,1,0:T(8,128)S(1)}, f32[24,8,128]{2,1,0:T(8,128)S(1)}) custom-call(f32[8,24,8,128]{3,2,1,0:T(8,128)} %solute.1, f32[24,8,128]{2,1,0:T(8,128)} %heat_hbm.1, f32[24,8,128]{2,1,0:T(8,128)} %east_hbm.1, f32[24,8,128]{2,1,0:T(8,128)} %north_hbm.1, s32[8,24]{1,0:T(8,128)} %bitcast.2, f32[16,16]{1,0:T(8,128)} %rates_hbm.1, ...), custom_call_target="tpu_custom_call" | custom-call | tf_op jit(solution)/shard_map/pallas_call | solution.py:896
  28.8 0.9 %shard_map.87 = (f32[8,24,8,128]{3,2,1,0:T(8,128)}, f32[24,8,128]{2,1,0:T(8,128)}) custom-call(f32[8,24,8,128]{3,2,1,0:T(8,128)S(1)} %get-tuple-element.4.mixture, f32[24,8,128]{2,1,0:T(8,128)S(1)} %get-tuple-element.5.heat), custom_call_target="tpu_custom_call" | custom-call | tf_op jit(solution)/shard_map/pallas_call | solution.py:921
